TPU v7x, 32 devices: a whole 2x2x4 slice. The times are simulated.
32 devices in a mesh: fsdp: 8 (over y, x, core), dp: 4 (over z).
Axes of the slice: x: 2, y: 2, z: 4, core: 2. Of those that a mesh axis runs over, the one named last changes fastest.
Arguments:
- hidden: bfloat16 [8192, 14336], P(('fsdp', 'dp')), may hold values from -6 to 6
- cotangent: bfloat16 [8192, 4096], P(('fsdp', 'dp')), may hold values from -6 to 6
- tiles: bfloat16 [64, 128, 128], P('fsdp'), may hold values from -0.25 to 0.25
- tile_rows: int32 [64], P('fsdp'), may hold values from 0 to 111, as said below
- tile_cols: int32 [64], P('fsdp'), may hold values from 0 to 31, as said below
- counts: int32 [8], P('fsdp'), may hold values from 1 to 8, as said below
Outputs:
- layer_out: bfloat16 [8192, 4096], P(('fsdp', 'dp'))
- hidden_grad: bfloat16 [8192, 14336], P(('fsdp', 'dp'))
- weight_grad: float32 [64, 128, 128], P('fsdp')
Inputs may be any that keep to these rules, and one draw needn't show every extreme that they name: `tile_rows`: every slot (live or not) names a different block; the row block is below 112. `tile_cols`: the column block is below 32. `counts`: some owner has all 8 slots live in every draw.
All inputs are finite; a program needn't handle non-finite values.
Results may differ from a plain program's by a relative error of at most 0.0085.
Values may be sent and summed in bfloat16 or wider, within the bound.
A program may use at most 192 MiB of HBM per device.

v0:
```python
import math
import jax
import jax.numpy as jnp
from jax import lax
from jax.sharding import PartitionSpec as P


def one_hot_of(ids, width):
    return (ids[:, None] == jnp.arange(width, dtype=jnp.int32)[None, :]).astype(jnp.bfloat16)


def select_blocks(blocks, ids):
    table = one_hot_of(ids, blocks.shape[1])
    chosen = jnp.einsum("tbe,kb->tke", blocks, table, preferred_element_type=jnp.float32)
    return chosen.astype(jnp.bfloat16)


def place_blocks(partial_value, ids, width):
    table = one_hot_of(ids, width).astype(jnp.float32)
    return jnp.einsum("tke,kb->tbe", partial_value, table)


def shards(hidden, cotangent, tiles, tile_rows, tile_cols, counts):
    tokens = hidden.shape[0]
    slots_own = tiles.shape[0]
    edge_len = tiles.shape[1]
    blocks_ff = hidden.shape[1] // edge_len
    blocks_model = cotangent.shape[1] // edge_len
    live_slots = jnp.arange(slots_own) < counts[0]
    masked = jnp.where(live_slots[:, None, None], tiles, jnp.zeros_like(tiles))
    all_rows, all_cols = (
        lax.all_gather(tile_rows, "fsdp", axis=0, tiled=True),
        lax.all_gather(tile_cols, "fsdp", axis=0, tiled=True),
    )
    hidden_blocks = hidden.reshape(tokens, blocks_ff, edge_len)
    upstream_blocks = cotangent.reshape(tokens, blocks_model, edge_len)
    gathered = lax.all_gather(masked, "fsdp", axis=0, tiled=True)
    row_ids = all_rows
    col_ids = all_cols
    picked = select_blocks(hidden_blocks, row_ids)
    partial_value = jnp.einsum("tkf,kfd->tkd", picked, gathered, preferred_element_type=jnp.float32)
    layer_acc = place_blocks(partial_value, col_ids, blocks_model)
    row_ids = all_rows
    col_ids = all_cols
    upstream = select_blocks(upstream_blocks, col_ids)
    partial_value = jnp.einsum(
        "tkd,kfd->tkf", upstream, gathered, preferred_element_type=jnp.float32
    )
    grad_acc = place_blocks(partial_value, row_ids, blocks_ff)
    row_ids = all_rows
    col_ids = all_cols
    picked = select_blocks(hidden_blocks, row_ids)
    upstream = select_blocks(upstream_blocks, col_ids)
    owned = lax.psum_scatter(
        jnp.einsum("tkf,tkd->kfd", picked, upstream, preferred_element_type=jnp.float32),
        "fsdp",
        scatter_dimension=0,
        tiled=True,
    )
    summed = lax.psum(owned, "dp")
    raw_grad = jnp.where(live_slots[:, None, None], summed, jnp.zeros_like(summed))
    local_squares = jnp.sum(raw_grad * raw_grad)
    local_entries = counts[0].astype(jnp.float32) * edge_len * edge_len
    squares, entries = lax.psum((local_squares, local_entries), "fsdp")
    spread = jnp.sqrt(squares / entries)
    root_tokens = math.sqrt(tokens * lax.axis_size("fsdp") * lax.axis_size("dp"))
    factor = jnp.minimum(1.0, 0.5 * root_tokens / spread) / root_tokens
    layer_out = layer_acc.reshape(tokens, blocks_model * edge_len).astype(jnp.bfloat16)
    hidden_grad = grad_acc.reshape(tokens, blocks_ff * edge_len).astype(jnp.bfloat16)
    return (layer_out, hidden_grad, raw_grad * factor)


def solution(mesh):
    placed = (
        P(("fsdp", "dp"), None),
        P(("fsdp", "dp"), None),
        P("fsdp", None, None),
        P("fsdp"),
        P("fsdp"),
        P("fsdp"),
    )
    return jax.shard_map(
        shards,
        mesh=mesh,
        in_specs=placed,
        out_specs=(P(("fsdp", "dp"), None), P(("fsdp", "dp"), None), P("fsdp", None, None)),
        check_vma=False,
    )
```

profile of v0, /device:TPU:0, one launch (start us, length us, event | category | flops | bytes accessed | tf_op | source)
XLA Modules:
  0.0 171.5 jit_solution(11835242717945344327)
XLA Ops:
  7.2 0.0 all-gather.2.cloned.1.call-start
  7.9 1.7 %broadcast_select_fusion = bf16[8,128,128]{2,1,0:T(8,128)(2,1)} fusion(bf16[8,128,128]{2,1,0:T(8,128)(2,1)} %param.8, pred[8]{0:T(512)(128)(4,1)S(1)} %iota_compare_fusion.2), kind=kLoop, calls=%fused_computation.16 | loop fusion | flops 131072 | bytes 524296 | tf_op jit(solution)/shard_map/jit(_where)/select_n | solution.py:30
  9.6 0.0 all-gather.2.cloned.1.call-update
  9.6 0.0 reduce-scatter.2.cloned.1.call-start
  9.7 0.0 copy-start.8
  9.7 0.0 copy-start.6
  9.7 0.0 copy-start.7
  9.7 7.8 %copy.16 = bf16[32,8,112,128]{3,2,1,0:T(8,128)(2,1)} copy(bf16[32,8,112,128]{3,1,2,0:T(8,128)(2,1)} %bitcast.50) | data formatting | bytes 14680064
  17.6 0.0 copy-done.8
  17.6 0.6 dynamic-slice
  18.7 0.0 copy-done.6
  18.7 0.2 dynamic-update-slice
  19.0 0.0 copy-done.7
  19.0 0.2 dynamic-update-slice.1
  19.2 9.7 %all-reduce.2 = (s32[64]{0:T(128)S(1)}, s32[64]{0:T(128)S(1)}) all-reduce(s32[64]{0:T(128)S(1)} %dynamic-update-slice.1, s32[64]{0:T(128)S(1)} %dynamic-update-slice), channel_id=1, replica_groups=mesh['fsdp'=8,'dp'=4] {'fsdp'}, use_global_device_ids=true, to_apply=%add.1 | all-reduce | flops 128 | bytes 1024
  28.9 6.4 %convert_bitcast_fusion.1 = bf16[256,64,128]{2,1,0:T(8,128)(2,1)} fusion(bf16[256,112,128]{2,1,0:T(8,128)(2,1)} %bitcast.46, s32[64]{0:T(128)S(1)} %get-tuple-element.3), kind=kOutput, calls=%fused_computation.7 | convolution fusion | flops 471866368 | bytes 11534592 | tf_op jit(solution)/shard_map/tbe,kb->tke/dot_general | solution.py:14
  35.3 0.0 copy-start.5
  35.3 7.1 %copy.11 = bf16[256,64,128]{0,2,1:T(8,128)(2,1)} copy(bf16[256,64,128]{2,1,0:T(8,128)(2,1)} %convert_bitcast_fusion.1) | data formatting | bytes 8388608 | tf_op jit(solution)/shard_map/convert_element_type | solution.py:15
  42.3 0.0 copy-done.5
  42.3 0.5 copy.18
  42.8 0.0 copy-start
  42.8 1.3 convert_bitcast_fusion
  44.1 0.0 copy-start.1
  44.1 2.0 %copy-done.1 = bf16[256,64,128]{2,1,0:T(8,128)(2,1)} copy-done((bf16[256,64,128]{2,1,0:T(8,128)(2,1)}, bf16[256,64,128]{2,1,0:T(8,128)(2,1)S(1)}, u32[]{:S(2)}) %copy-start.1) | copy-done | bytes 4194328
  46.1 0.0 copy-done
  46.1 7.2 %fusion.9 = f32[64,128,128]{2,1,0:T(8,128)} fusion(bf16[256,64,128]{0,2,1:T(8,128)(2,1)S(1)} %copy-done, bf16[256,64,128]{2,1,0:T(8,128)(2,1)S(1)} %convert_bitcast_fusion), kind=kOutput, calls=%fused_computation.10 | convolution fusion | flops 536870912 | bytes 12582912 | tf_op jit(solution)/shard_map/tkf,tkd->kfd/dot_general | solution.py:55
  53.3 0.0 reduce-scatter.2.cloned.1.call-update
  53.4 0.2 all-reduce.6.cloned.1.call-start
  53.6 0.0 all-gather.2.cloned.1.call-done
  53.6 9.4 %fusion.7 = bf16[64,128,256]{2,1,0:T(8,128)(2,1)} fusion(bf16[64,128,128]{2,1,0:T(8,128)(2,1)} %all-gather.2.cloned.1.call-done, bf16[256,64,128]{2,1,0:T(8,128)(2,1)} %copy-done.1), kind=kOutput, calls=%fused_computation.8 | convolution fusion | flops 536870912 | bytes 10485760 | tf_op jit(solution)/shard_map/tkd,kfd->tkf/dot_general | solution.py:46
  63.0 6.6 %copy.15 = bf16[64,128,256]{1,0,2:T(8,128)(2,1)} copy(bf16[64,128,256]{2,1,0:T(8,128)(2,1)} %fusion.7) | data formatting | bytes 8388608 | tf_op jit(solution)/shard_map/tkd,kfd->tkf/dot_general | solution.py:46
  69.7 0.0 copy-start.3
  69.7 7.6 %fusion.4 = bf16[112,256,128]{2,0,1:T(8,128)(2,1)} fusion(bf16[64,128,256]{1,0,2:T(8,128)(2,1)} %copy.15, s32[64]{0:T(128)S(1)} %get-tuple-element.3), kind=kOutput, calls=%fused_computation.5 | convolution fusion | flops 469769216 | bytes 11534592 | tf_op jit(solution)/shard_map/tke,kb->tbe/dot_general | solution.py:20
  77.3 26.8 %reduce-scatter.2.cloned.1.call-done = f32[8,128,128]{2,1,0:T(8,128)} async-done(((f32[64,128,128]{2,1,0:T(8,128)}), f32[8,128,128]{2,1,0:T(8,128)}) %reduce-scatter.2.cloned.1.call-update) | async-done | bytes 524304 | tf_op jit(solution)/shard_map/reduce_scatter | solution.py:54
  104.1 0.0 all-reduce.6.cloned.1.call-update
  104.1 0.0 copy-done.3
  104.1 0.0 copy-start.2
  104.1 5.6 %fusion.24 = bf16[64,128,256]{2,1,0:T(8,128)(2,1)} fusion(bf16[64,128,128]{2,1,0:T(8,128)(2,1)S(1)} %copy-done.3, bf16[256,64,128]{0,2,1:T(8,128)(2,1)} %copy.11), kind=kOutput, calls=%fused_computation.26 | convolution fusion | flops 536870912 | bytes 10485760 | tf_op jit(solution)/shard_map/tkf,kfd->tkd/dot_general | solution.py:41
  109.8 0.0 copy-done.2
  109.8 4.9 %copy.26 = bf16[32,8,112,128]{3,1,2,0:T(8,128)(2,1)} copy(bf16[32,8,112,128]{3,2,1,0:T(8,128)(2,1)S(1)} %bitcast.47) | data formatting | bytes 14680064
  114.7 6.5 %copy.13 = bf16[64,128,256]{1,0,2:T(8,128)(2,1)} copy(bf16[64,128,256]{2,1,0:T(8,128)(2,1)} %fusion.24) | data formatting | bytes 8388608 | tf_op jit(solution)/shard_map/tkf,kfd->tkd/dot_general | solution.py:41
  121.2 2.9 %fusion.11 = bf16[32,256,128]{2,0,1:T(8,128)(2,1)S(1)} fusion(bf16[64,128,256]{1,0,2:T(8,128)(2,1)} %copy.13, s32[64]{0:T(128)S(1)} %get-tuple-element.4), kind=kOutput, calls=%fused_computation.13 | convolution fusion | flops 134219776 | bytes 6291712 | tf_op jit(solution)/shard_map/tke,kb->tbe/dot_general | solution.py:20
  124.1 21.0 %all-reduce.6.cloned.1.call-done = f32[8,128,128]{2,1,0:T(8,128)} async-done(((f32[8,128,128]{2,1,0:T(8,128)}), f32[8,128,128]{2,1,0:T(8,128)}) %all-reduce.6.cloned.1.call-update) | async-done | bytes 524304 | tf_op jit(solution)/shard_map/psum | solution.py:60
  145.2 0.0 copy-start.4
  145.2 1.9 %multiply_reduce_fusion = f32[]{:T(128)} fusion(f32[8,128,128]{2,1,0:T(8,128)} %all-reduce.6.cloned.1.call-done, pred[8]{0:T(512)(128)(4,1)S(1)} %iota_compare_fusion.2), kind=kLoop, calls=%fused_computation.14 | loop fusion | flops 393215 | bytes 524300 | tf_op jit(solution)/shard_map/reduce_sum | solution.py:62
  147.1 2.3 %copy.27 = bf16[32,8,32,128]{3,1,2,0:T(8,128)(2,1)} copy(bf16[32,8,32,128]{3,2,1,0:T(8,128)(2,1)S(1)} %bitcast.48) | data formatting | bytes 4194304
  149.4 13.3 %all-reduce.3 = (f32[]{:T(128)}, f32[]{:T(128)}) all-reduce(f32[]{:T(128)} %multiply_reduce_fusion, f32[]{:T(128)S(6)} %mul.14), channel_id=1, replica_groups=mesh['fsdp'=8,'dp'=4] {'fsdp'}, use_global_device_ids=true, to_apply=%region_3.4 | all-reduce | flops 2 | bytes 16 | tf_op jit(solution)/shard_map/psum | solution.py:64
  164.0 0.0 copy-done.4
  164.0 0.9 select_multiply_fusion
  (3 shorter events, 0.0 us)
Async XLA Ops:
  7.2 46.5 %all-gather.2.cloned.1.call-start = ((), (), s32[]{:S(2)}) async-start(), calls=%async_computation.1 | async-start | bytes 2359296 | tf_op jit(solution)/shard_map/all_gather | solution.py:37
  9.6 94.5 %reduce-scatter.2.cloned.1.call-start = ((), (), s32[]{:S(2)}) async-start(), calls=%async_computation.2 | async-start | bytes 4718592 | tf_op jit(solution)/shard_map/reduce_scatter | solution.py:54
  9.7 7.9 %copy-start.8 = (u32[32]{0:T(128)S(1)}, u32[32]{0:T(128)}, u32[]{:S(2)}) copy-start(u32[32]{0:T(128)} %constant.18) | copy-start | bytes 388
  9.7 9.0 %copy-start.6 = (s32[8]{0:T(128)S(1)}, s32[8]{0:T(128)}, u32[]{:S(2)}) copy-start(s32[8]{0:T(128)} %param.10) | copy-start | bytes 100
  9.7 9.3 %copy-start.7 = (s32[8]{0:T(128)S(1)}, s32[8]{0:T(128)}, u32[]{:S(2)}) copy-start(s32[8]{0:T(128)} %param.9) | copy-start | bytes 100
  35.3 7.1 %copy-start.5 = (bf16[256,4096]{1,0:T(8,128)(2,1)S(1)}, bf16[256,4096]{1,0:T(8,128)(2,1)}, u32[]{:S(2)}) copy-start(bf16[256,4096]{1,0:T(8,128)(2,1)} %param.7) | copy-start | bytes 6291460
  42.8 3.3 %copy-start = (bf16[256,64,128]{0,2,1:T(8,128)(2,1)S(1)}, bf16[256,64,128]{0,2,1:T(8,128)(2,1)}, u32[]{:S(2)}) copy-start(bf16[256,64,128]{0,2,1:T(8,128)(2,1)} %copy.11) | copy-start | bytes 12582916
  44.1 2.0 %copy-start.1 = (bf16[256,64,128]{2,1,0:T(8,128)(2,1)}, bf16[256,64,128]{2,1,0:T(8,128)(2,1)S(1)}, u32[]{:S(2)}) copy-start(bf16[256,64,128]{2,1,0:T(8,128)(2,1)S(1)} %convert_bitcast_fusion) | copy-start | bytes 12582916
  53.4 91.8 %all-reduce.6.cloned.1.call-start = ((), (), s32[]{:S(2)}) async-start(), calls=%async_computation.3 | async-start | bytes 1048576 | tf_op jit(solution)/shard_map/psum | solution.py:60
  69.7 34.5 %copy-start.3 = (bf16[64,128,128]{2,1,0:T(8,128)(2,1)S(1)}, bf16[64,128,128]{2,1,0:T(8,128)(2,1)}, u32[]{:S(2)}) copy-start(bf16[64,128,128]{2,1,0:T(8,128)(2,1)} %all-gather.2.cloned.1.call-done) | copy-start | bytes 6291460
  104.1 5.6 %copy-start.2 = (bf16[112,256,128]{2,0,1:T(8,128)(2,1)S(1)}, bf16[112,256,128]{2,0,1:T(8,128)(2,1)}, u32[]{:S(2)}) copy-start(bf16[112,256,128]{2,0,1:T(8,128)(2,1)} %fusion.4) | copy-start | bytes 22020100
  145.2 18.9 %copy-start.4 = (f32[8,128,128]{2,1,0:T(8,128)S(1)}, f32[8,128,128]{2,1,0:T(8,128)}, u32[]{:S(2)}) copy-start(f32[8,128,128]{2,1,0:T(8,128)} %all-reduce.6.cloned.1.call-done) | copy-start | bytes 1572868
Sparse Core Ops, SparseCore 0:
  10.4 30.5 all-gather.1
  53.5 50.5 reduce-scatter.1
  106.4 38.6 all-reduce.5
where the time goes:
time: 172 us; the launch traced here: 171 us
  waiting for transfers between devices  47.9 us (28%)
  matrix products  40.4 us (23%)
  local copies, waits for them, and re-layouts  38.9 us (23%)
  blocking collectives  23 us (13%)
  between operations  16.4 us (10%)
  other arithmetic  4.57 us (3%)
    reduce_scatter x1, waiting for transfers between devices, shards(): lax.psum_scatter(jnp.einsum('tkf,tkd->kfd', picked, upstream, preferred_e...  26.8 us
    psum x1, waiting for transfers between devices, shards(): summed = lax.psum(owned, 'dp')  21 us
    unnamed x27, local copies, waits for them, and re-layouts  18.6 us
    psum x1, blocking collectives, shards(): squares, entries = lax.psum((local_squares, local_entries), 'fsdp')  13.3 us
    dot_general x2, matrix products, place_blocks(): return jnp.einsum('tke,kb->tbe', partial_value, table)  10.5 us
    unnamed x1, blocking collectives  9.69 us
    dot_general x1, matrix products, shards(): jnp.einsum('tkd,kfd->tkf', upstream, gathered, preferred_element_type=jnp...  9.41 us
    dot_general x2, matrix products, select_blocks(): jnp.einsum('tbe,kb->tke', blocks, table, preferred_element_type=jnp.float32)  7.66 us
  transfers between devices with their start and end apart: 3, of which 2 were waited for; matrix products, arithmetic and copies ran while one was open for 44% of the time, Pallas kernels for 0%

commit v1 on v0

--- a/solution.py
+++ b/solution.py
@@ -57,7 +57,8 @@
         scatter_dimension=0,
         tiled=True,
     )
-    summed = lax.psum(owned, "dp")
+    mixed_arr = lax.all_gather(owned, axis_name="dp")
+    summed = jnp.sum(mixed_arr, axis=0)
     raw_grad = jnp.where(live_slots[:, None, None], summed, jnp.zeros_like(summed))
     local_squares = jnp.sum(raw_grad * raw_grad)
     local_entries = counts[0].astype(jnp.float32) * edge_len * edge_len

time: 172 us -> 208 us (1.21)
  waiting for transfers between devices: 47.9 us -> 87 us
  matrix products: 40.4 us -> 36.4 us
    all_gather x1, waiting for transfers between devices: 0.02 us -> 30.2 us  [shards(): gathered = lax.all_gather(masked, 'fsdp', axis=0, tiled=True)]
    reduce_scatter x1, waiting for transfers between devices: 26.8 us -> 49 us  [shards(): lax.psum_scatter(jnp.einsum('tkf,tkd->kfd', picked, upstream, preferred_e...]
    psum x1 -> x0, waiting for transfers between devices: 21 us -> none  [shards(): summed = lax.psum(owned, 'dp')]
    all_gather x0 -> x1, waiting for transfers between devices: none -> 7.67 us  [shards(): mixed_arr = lax.all_gather(owned, axis_name='dp')]
    dot_general x2, matrix products: 10.5 us -> 7.26 us  [place_blocks(): return jnp.einsum('tke,kb->tbe', partial_value, table)]
    unnamed x27 -> x25, local copies, waits for them, and re-layouts: 18.6 us -> 18.8 us
  transfers between devices with their start and end apart: 3 -> 3, of which waited for: 2 -> 3; matrix products, arithmetic and copies ran while one was open for 44% -> 19% of each run, Pallas kernels for 0% -> 0%
where the time goes in v1:
time: 208 us; the launch traced here: 207 us
  waiting for transfers between devices  87 us (42%)
  local copies, waits for them, and re-layouts  39 us (19%)
  matrix products  36.4 us (18%)
  blocking collectives  23.6 us (11%)
  between operations  16.6 us (8%)
  other arithmetic  4.27 us (2%)
    reduce_scatter x1, waiting for transfers between devices, shards(): lax.psum_scatter(jnp.einsum('tkf,tkd->kfd', picked, upstream, preferred_e...  49 us
    all_gather x1, waiting for transfers between devices, shards(): gathered = lax.all_gather(masked, 'fsdp', axis=0, tiled=True)  30.2 us
    unnamed x25, local copies, waits for them, and re-layouts  18.8 us
    psum x1, blocking collectives, shards(): squares, entries = lax.psum((local_squares, local_entries), 'fsdp')  14.1 us
    unnamed x1, blocking collectives  9.49 us
    dot_general x1, matrix products, shards(): jnp.einsum('tkd,kfd->tkf', upstream, gathered, preferred_element_type=jnp...  9.42 us
    all_gather x1, waiting for transfers between devices, shards(): mixed_arr = lax.all_gather(owned, axis_name='dp')  7.67 us
    dot_general x2, matrix products, select_blocks(): jnp.einsum('tbe,kb->tke', blocks, table, preferred_element_type=jnp.float32)  7.64 us
  transfers between devices with their start and end apart: 3, of which 3 were waited for; matrix products, arithmetic and copies ran while one was open for 19% of the time, Pallas kernels for 0%

profile of v1, /device:TPU:0, one launch (start us, length us, event | category | flops | bytes accessed | tf_op | source)
XLA Modules:
  0.0 207.0 jit_solution(13357291266326853443)
XLA Ops:
  7.2 0.0 reduce-scatter.2.cloned.1.call-start
  7.2 0.0 copy-start.7
  7.2 0.0 copy-start.5
  7.2 0.0 copy-start.6
  7.3 7.8 %copy.16 = bf16[32,8,112,128]{3,2,1,0:T(8,128)(2,1)} copy(bf16[32,8,112,128]{3,1,2,0:T(8,128)(2,1)} %bitcast.51) | data formatting | bytes 14680064
  15.1 0.0 copy-done.7
  15.1 0.6 dynamic-slice
  16.3 0.0 copy-done.5
  16.4 0.2 dynamic-update-slice
  16.6 0.0 copy-done.6
  16.6 0.2 dynamic-update-slice.1
  16.8 9.5 %all-reduce.2 = (s32[64]{0:T(128)S(1)}, s32[64]{0:T(128)S(1)}) all-reduce(s32[64]{0:T(128)S(1)} %dynamic-update-slice.1, s32[64]{0:T(128)S(1)} %dynamic-update-slice), channel_id=1, replica_groups=mesh['fsdp'=8,'dp'=4] {'fsdp'}, use_global_device_ids=true, to_apply=%add.1 | all-reduce | flops 128 | bytes 1024
  26.3 6.3 %convert_bitcast_fusion.1 = bf16[256,64,128]{2,1,0:T(8,128)(2,1)} fusion(bf16[256,112,128]{2,1,0:T(8,128)(2,1)} %bitcast.47, s32[64]{0:T(128)S(1)} %get-tuple-element.3), kind=kOutput, calls=%fused_computation.7 | convolution fusion | flops 471866368 | bytes 11534592 | tf_op jit(solution)/shard_map/tbe,kb->tke/dot_general | solution.py:14
  32.7 0.0 copy-start.3
  32.7 7.0 %copy.11 = bf16[256,64,128]{0,2,1:T(8,128)(2,1)} copy(bf16[256,64,128]{2,1,0:T(8,128)(2,1)} %convert_bitcast_fusion.1) | data formatting | bytes 8388608 | tf_op jit(solution)/shard_map/convert_element_type | solution.py:15
  39.7 0.0 copy-done.3
  39.7 0.5 copy.18
  40.2 0.0 copy-start
  40.2 1.3 convert_bitcast_fusion
  41.5 0.0 copy-start.2
  41.5 2.0 copy-done.2
  43.5 0.0 copy-done
  43.5 7.2 %fusion.9 = f32[64,128,128]{2,1,0:T(8,128)} fusion(bf16[256,64,128]{0,2,1:T(8,128)(2,1)S(1)} %copy-done, bf16[256,64,128]{2,1,0:T(8,128)(2,1)S(1)} %convert_bitcast_fusion), kind=kOutput, calls=%fused_computation.10 | convolution fusion | flops 536870912 | bytes 12582912 | tf_op jit(solution)/shard_map/tkf,tkd->kfd/dot_general | solution.py:55
  50.7 0.0 copy-start.4
  50.7 0.0 reduce-scatter.2.cloned.1.call-update
  50.7 0.0 all-gather.4.cloned.1.call-start
  51.5 0.2 copy-done.4
  51.7 0.8 broadcast_select_fusion
  52.5 0.0 all-gather.4.cloned.1.call-update
  52.5 0.2 all-gather.6.cloned.1.call-start
  52.7 49.0 %reduce-scatter.2.cloned.1.call-done = f32[8,128,128]{2,1,0:T(8,128)} async-done(((f32[64,128,128]{2,1,0:T(8,128)}), f32[8,128,128]{2,1,0:T(8,128)}) %reduce-scatter.2.cloned.1.call-update) | async-done | bytes 524304 | tf_op jit(solution)/shard_map/reduce_scatter | solution.py:54
  101.7 0.0 all-gather.6.cloned.1.call-update
  101.8 30.2 %all-gather.4.cloned.1.call-done = bf16[64,128,128]{2,1,0:T(8,128)(2,1)} async-done(((bf16[8,128,128]{2,1,0:T(8,128)(2,1)}), bf16[64,128,128]{2,1,0:T(8,128)(2,1)}) %all-gather.4.cloned.1.call-update) | async-done | bytes 2097168 | tf_op jit(solution)/shard_map/all_gather | solution.py:37
  132.0 9.4 %fusion.7 = bf16[64,128,256]{2,1,0:T(8,128)(2,1)} fusion(bf16[64,128,128]{2,1,0:T(8,128)(2,1)} %all-gather.4.cloned.1.call-done, bf16[256,64,128]{2,1,0:T(8,128)(2,1)} %copy-done.2), kind=kOutput, calls=%fused_computation.8 | convolution fusion | flops 536870912 | bytes 10485760 | tf_op jit(solution)/shard_map/tkd,kfd->tkf/dot_general | solution.py:46
  141.4 6.5 %copy.15 = bf16[64,128,256]{1,0,2:T(8,128)(2,1)} copy(bf16[64,128,256]{2,1,0:T(8,128)(2,1)} %fusion.7) | data formatting | bytes 8388608 | tf_op jit(solution)/shard_map/tkd,kfd->tkf/dot_general | solution.py:46
  147.9 4.4 %fusion.4 = bf16[112,256,128]{2,0,1:T(8,128)(2,1)S(1)} fusion(bf16[64,128,256]{1,0,2:T(8,128)(2,1)} %copy.15, s32[64]{0:T(128)S(1)} %get-tuple-element.3), kind=kOutput, calls=%fused_computation.5 | convolution fusion | flops 469769216 | bytes 11534592 | tf_op jit(solution)/shard_map/tke,kb->tbe/dot_general | solution.py:20
  152.3 0.0 copy-start.1
  152.3 4.9 %copy.26 = bf16[32,8,112,128]{3,1,2,0:T(8,128)(2,1)} copy(bf16[32,8,112,128]{3,2,1,0:T(8,128)(2,1)S(1)} %bitcast.48) | data formatting | bytes 14680064
  157.2 0.0 copy-done.1
  157.3 4.8 %fusion.24 = bf16[64,128,256]{2,1,0:T(8,128)(2,1)} fusion(bf16[64,128,128]{2,1,0:T(8,128)(2,1)} %all-gather.4.cloned.1.call-done, bf16[256,64,128]{0,2,1:T(8,128)(2,1)S(1)} %copy-done.1), kind=kOutput, calls=%fused_computation.26 | convolution fusion | flops 536870912 | bytes 10485760 | tf_op jit(solution)/shard_map/tkf,kfd->tkd/dot_general | solution.py:41
  162.1 6.6 %copy.13 = bf16[64,128,256]{1,0,2:T(8,128)(2,1)} copy(bf16[64,128,256]{2,1,0:T(8,128)(2,1)} %fusion.24) | data formatting | bytes 8388608 | tf_op jit(solution)/shard_map/tkf,kfd->tkd/dot_general | solution.py:41
  168.7 2.9 %fusion.11 = bf16[32,256,128]{2,0,1:T(8,128)(2,1)S(1)} fusion(bf16[64,128,256]{1,0,2:T(8,128)(2,1)} %copy.13, s32[64]{0:T(128)S(1)} %get-tuple-element.4), kind=kOutput, calls=%fused_computation.13 | convolution fusion | flops 134219776 | bytes 6291712 | tf_op jit(solution)/shard_map/tke,kb->tbe/dot_general | solution.py:20
  171.6 7.7 %all-gather.6.cloned.1.call-done = f32[32,128,128]{2,1,0:T(8,128)} async-done(((f32[8,128,128]{2,1,0:T(8,128)}), f32[32,128,128]{2,1,0:T(8,128)}) %all-gather.6.cloned.1.call-update) | async-done | bytes 2097168 | tf_op jit(solution)/shard_map/all_gather | solution.py:60
  179.3 1.8 reduce_sum.18
  181.0 0.8 multiply_reduce_fusion
  181.8 2.3 %copy.27 = bf16[32,8,32,128]{3,1,2,0:T(8,128)(2,1)} copy(bf16[32,8,32,128]{3,2,1,0:T(8,128)(2,1)S(1)} %bitcast.49) | data formatting | bytes 4194304
  184.1 14.1 %all-reduce.3 = (f32[]{:T(128)}, f32[]{:T(128)}) all-reduce(f32[]{:T(128)} %multiply_reduce_fusion, f32[]{:T(128)S(6)} %mul.14), channel_id=1, replica_groups=mesh['fsdp'=8,'dp'=4] {'fsdp'}, use_global_device_ids=true, to_apply=%region_3.4 | all-reduce | flops 2 | bytes 16 | tf_op jit(solution)/shard_map/psum | solution.py:65
  199.6 0.9 select_multiply_fusion
  (3 shorter events, 0.0 us)
Async XLA Ops:
  7.2 94.6 %reduce-scatter.2.cloned.1.call-start = ((), (), s32[]{:S(2)}) async-start(), calls=%async_computation.2 | async-start | bytes 4718592 | tf_op jit(solution)/shard_map/reduce_scatter | solution.py:54
  7.2 7.9 %copy-start.7 = (u32[32]{0:T(128)S(1)}, u32[32]{0:T(128)}, u32[]{:S(2)}) copy-start(u32[32]{0:T(128)} %constant.18) | copy-start | bytes 388
  7.2 9.1 %copy-start.5 = (s32[8]{0:T(128)S(1)}, s32[8]{0:T(128)}, u32[]{:S(2)}) copy-start(s32[8]{0:T(128)} %param.10) | copy-start | bytes 100
  7.2 9.4 %copy-start.6 = (s32[8]{0:T(128)S(1)}, s32[8]{0:T(128)}, u32[]{:S(2)}) copy-start(s32[8]{0:T(128)} %param.9) | copy-start | bytes 100
  32.7 7.1 %copy-start.3 = (bf16[256,4096]{1,0:T(8,128)(2,1)S(1)}, bf16[256,4096]{1,0:T(8,128)(2,1)}, u32[]{:S(2)}) copy-start(bf16[256,4096]{1,0:T(8,128)(2,1)} %param.7) | copy-start | bytes 6291460
  40.2 3.3 %copy-start = (bf16[256,64,128]{0,2,1:T(8,128)(2,1)S(1)}, bf16[256,64,128]{0,2,1:T(8,128)(2,1)}, u32[]{:S(2)}) copy-start(bf16[256,64,128]{0,2,1:T(8,128)(2,1)} %copy.11) | copy-start | bytes 12582916
  41.5 2.0 copy-start.2
  50.7 0.9 copy-start.4
  50.7 81.3 %all-gather.4.cloned.1.call-start = ((), (), s32[]{:S(2)}) async-start(), calls=%async_computation.1 | async-start | bytes 2359296 | tf_op jit(solution)/shard_map/all_gather | solution.py:37
  52.5 126.8 %all-gather.6.cloned.1.call-start = ((), (), s32[]{:S(2)}) async-start(), calls=%async_computation.3 | async-start | bytes 2621440 | tf_op jit(solution)/shard_map/all_gather | solution.py:60
  152.3 5.0 %copy-start.1 = (bf16[256,64,128]{0,2,1:T(8,128)(2,1)S(1)}, bf16[256,64,128]{0,2,1:T(8,128)(2,1)}, u32[]{:S(2)}) copy-start(bf16[256,64,128]{0,2,1:T(8,128)(2,1)} %copy.11) | copy-start | bytes 12582916
Sparse Core Ops, SparseCore 0:
  50.9 50.8 reduce-scatter.1
  104.2 27.7 all-gather.3
  133.6 45.6 all-gather.5
